TPU v7x, 512 devices: a whole 4x4x16 slice. The times are simulated.
512 devices in a mesh: call: 64 (over z, y_hi, core), tensor: 8 (over x, y_lo).
Axes of the slice: x: 4, y: 4 (y_hi: 2, y_lo: 2; y = y_hi * 2 + y_lo), z: 16, core: 2. Of those that a mesh axis runs over, the one named last changes fastest.
Arguments:
- queries: bfloat16 [64, 768, 8192], P('call', None, 'tensor'), may hold values from -8 to 8
- child_kv: bfloat16 [64, 2, 768, 1024], P('call', None, None, 'tensor'), may hold values from -6 to 6
- summ_kv: bfloat16 [64, 2, 256, 1024], P('call', None, None, 'tensor'), may hold values from -6 to 6
- instr_pool: bfloat16 [64, 1024, 2, 1024], P('call', 'tensor'), may hold values from -16 to 16
- child_len: int32 [64], P('call'), may hold values from 256 to 768, as said below
- summ_len: int32 [64], P('call'), may hold values from 64 to 256, as said below
- owner_group: int32 [1], replicated, may hold values from 0 to 63
Outputs:
- attended: bfloat16 [64, 768, 8192], P('call', None, 'tensor')
Inputs may be any that keep to these rules, and one draw needn't show every extreme that they name: `child_len`: one call has exactly 768 child tokens and one exactly 256. `summ_len`: one call has exactly 256 summary tokens and one exactly 64.
All inputs are finite; a program needn't handle non-finite values.
Results may differ from a plain program's by a relative error of at most 0.006.
Values may be sent and summed in bfloat16 or wider, within the bound.
A program may use at most 64 MiB of HBM per device.

v0:
```python
import math

import jax
import jax.numpy as jnp
from jax import lax
from jax.sharding import PartitionSpec as P

HD = 128


NEG = -1e30


def broadcast(value, axis, source):
    kept = jnp.where(lax.axis_index(axis) == source, value, 0).astype(value.dtype)
    return lax.psum(kept, axis)


def passed_along(block, axis, distance):
    devices = range(lax.axis_size(axis))
    route = [(i - distance, i) for i in devices if i - distance in devices]
    return lax.ppermute(block, axis, route)


def head_split(packed, heads):
    total = packed.shape[0]
    width = packed.shape[1]
    return packed.reshape(total, heads, width // heads).transpose(1, 0, 2)


def partial_softmax(query_head, key_rows, value_rows, allowed):
    score_scale = 1.0 / math.sqrt(query_head.shape[1])
    scores = (
        lax.dot_general(
            query_head, key_rows, (((1,), (1,)), ((), ())), preferred_element_type=jnp.float32
        )
        * score_scale
    )
    scores = jnp.where(allowed, scores, NEG)
    maxima = jnp.max(scores, axis=1, keepdims=True)
    expons = jnp.where(allowed, jnp.exp(scores - maxima), 0.0)
    totals = jnp.sum(expons, axis=1, keepdims=True)
    weights = expons.astype(jnp.bfloat16)
    return (maxima, totals, jnp.dot(weights, value_rows, preferred_element_type=jnp.float32))


def over_heads(query_heads, key_heads, value_heads, allowed):
    group = query_heads.shape[0] // key_heads.shape[0]

    def single(pair):
        query_head, number = pair
        key_rows = lax.dynamic_index_in_dim(key_heads, number // group, 0, keepdims=False)
        value_rows = lax.dynamic_index_in_dim(value_heads, number // group, 0, keepdims=False)
        return partial_softmax(query_head, key_rows, value_rows, allowed)

    return lax.map(single, (query_heads, jnp.arange(query_heads.shape[0], dtype=jnp.int32)))


def shards(queries, child_kv, summ_kv, instr_pool, child_len, summ_len, owner_group):
    query_mat = queries[0]
    length = query_mat.shape[0]
    heads = query_mat.shape[1] // HD
    kv_heads = child_kv.shape[3] // HD
    fetched = broadcast(instr_pool, "call", owner_group[0])
    instr_local = lax.all_to_all(fetched, "tensor", split_axis=3, concat_axis=1, tiled=True)
    sibling_kv, sibling_len = passed_along((summ_kv, summ_len), "call", 1)
    instr_count = instr_local.shape[1]
    summ_count = summ_kv.shape[2]
    positions = jnp.arange(length, dtype=jnp.int32)
    own_allowed = positions[None, :] <= positions[:, None]
    remote_allowed = jnp.concatenate(
        [
            jnp.ones((length, instr_count), bool),
            jnp.broadcast_to(
                jnp.arange(summ_count, dtype=jnp.int32)[None, :] < sibling_len[0],
                (length, summ_count),
            ),
        ],
        1,
    )
    remote_keys = jnp.concatenate([instr_local[0, :, 0], sibling_kv[0, 0]], 0)
    remote_values = jnp.concatenate([instr_local[0, :, 1], sibling_kv[0, 1]], 0)
    query_heads = head_split(query_mat, heads)
    key_all = jnp.concatenate([remote_keys, child_kv[0, 0]], 0)
    value_all = jnp.concatenate([remote_values, child_kv[0, 1]], 0)
    allowed = jnp.concatenate([remote_allowed, own_allowed], 1)
    maxima, totals, sums = over_heads(
        query_heads, head_split(key_all, kv_heads), head_split(value_all, kv_heads), allowed
    )
    combined = sums / totals
    result = combined.transpose(1, 0, 2).reshape(length, heads * HD)
    result = jnp.where((positions < child_len[0])[:, None], result, 0.0)
    return result.astype(jnp.bfloat16)[None]


def solution(mesh):
    in_specs = (
        P("call", None, "tensor"),
        P("call", None, None, "tensor"),
        P("call", None, None, "tensor"),
        P("call", "tensor", None, None),
        P("call"),
        P("call"),
        P(),
    )
    out_specs = P("call", None, "tensor")
    return jax.shard_map(shards, mesh=mesh, in_specs=in_specs, out_specs=out_specs, check_vma=False)
```

profile of v0, /device:TPU:1, one launch (start us, length us, event | category | flops | bytes accessed | tf_op | source)
XLA Modules:
  0.0 634.7 jit_solution(1127240871721148693)
XLA Ops:
  6.5 2.8 copy.22
  11.2 6.2 collective-permute-start
  19.6 2.6 copy.21
  23.5 526.0 %all-reduce.2.cloned.1.call-done = bf16[1,128,2,1024]{1,2,0,3:T(2,128)(2,1)} async-done(((bf16[1,128,2,1024]{1,2,0,3:T(2,128)(2,1)}), bf16[1,128,2,1024]{1,2,0,3:T(2,128)(2,1)}) %all-reduce.2.cloned.1.call-update) | async-done | bytes 524304 | tf_op jit(solution)/shard_map/psum | solution.py:16
  549.5 4.0 all-to-all-start
  554.1 8.0 %all-to-all-done = bf16[1,128,2,1024]{1,2,0,3:T(2,128)(2,1)S(1)} async-done(((bf16[1,128,2,1024]{1,2,0,3:T(2,128)(2,1)}), bf16[1,128,2,1024]{1,2,0,3:T(2,128)(2,1)S(1)}, u32[]{:S(2)}, u32[]{:S(2)}) %all-to-all-start) | async-done | bytes 524320 | tf_op jit(solution)/shard_map/all_to_all | solution.py:65
  562.7 59.4 %while.13 = (s32[]{:T(128)}, f32[8,768,1]{1,0,2:T(8,128)S(1)}, f32[8,768,128]{2,1,0:T(8,128)}, bf16[8,768,128]{1,2,0:T(8,128)(2,1)}, bf16[1,2048,128]{2,1,0:T(8,...) while((s32[]{:T(128)}, f32[8,768,1]{1,0,2:T(8,128)S(1)}, ...), condition=%wide.region_4.5_spmd, body=%wide.region_1.4_spmd.sunk | while | flops 825752064 | bytes 25257056 | solution.py:56
  562.8 2.5 fusion.27
  565.2 2.5 fusion.29
  567.8 2.3 fusion.28
  570.2 2.5 fusion.27
  572.7 2.5 fusion.29
  575.2 2.3 fusion.28
  577.6 2.5 fusion.27
  580.1 2.5 fusion.29
  582.6 2.3 fusion.28
  585.0 2.5 fusion.27
  587.5 2.5 fusion.29
  590.1 2.3 fusion.28
  592.5 2.5 fusion.27
  595.0 2.5 fusion.29
  597.5 2.3 fusion.28
  599.9 2.5 fusion.27
  602.4 2.5 fusion.29
  604.9 2.3 fusion.28
  607.3 2.5 fusion.27
  609.8 2.5 fusion.29
  612.4 2.3 fusion.28
  614.8 2.5 fusion.27
  617.3 2.5 fusion.29
  619.8 2.3 fusion.28
  622.2 2.4 divide_bitcast_fusion
  (40 shorter events, 9.1 us)
Async XLA Ops:
  6.5 543.0 %all-reduce.2.cloned.1.call-start = ((), (), s32[]{:S(2)}) async-start(), calls=%async_computation.1 | async-start | bytes 1048576 | tf_op jit(solution)/shard_map/psum | solution.py:16
  6.5 16.3 %copy-start = (bf16[1,2,768,128]{3,2,1,0:T(8,128)(2,1)S(1)}, bf16[1,2,768,128]{3,2,1,0:T(8,128)(2,1)}, u32[]{:S(2)}) copy-start(bf16[1,2,768,128]{3,2,1,0:T(8,128)(2,1)} %param.10) | copy-start | bytes 1179652
  11.2 542.9 %collective-permute-start = (bf16[1,2,256,128]{3,2,1,0:T(8,128)(2,1)}, bf16[1,2,256,128]{3,2,1,0:T(8,128)(2,1)S(1)}, u32[]{:S(2)}, u32[]{:S(2)}) collective-permute-start(bf16[1,2,256,128]{3,2,1,0:T(8,128)(2,1)} %param.11), channel_id=1, source_target_pairs={{0,8},{8,16},{16,24},{24,32},{32,40},{40,48},{48,56},{56,64},{64,7... | collective-permute-start | bytes 393224 | tf_op jit(solution)/shard_map/ppermute | solution.py:22
  17.4 5.4 collective-permute-start.1
  549.5 12.6 %all-to-all-start = ((bf16[1,128,2,1024]{1,2,0,3:T(2,128)(2,1)}), bf16[1,128,2,1024]{1,2,0,3:T(2,128)(2,1)S(1)}, u32[]{:S(2)}, u32[]{:S(2)}) async-start(bf16[1,128,2,1024]{1,2,0,3:T(2,128)(2,1)} %all-reduce.2.cloned.1.call-done), calls=%async_computation | async-start | bytes 1048576 | tf_op jit(solution)/shard_map/all_to_all | solution.py:65
Sparse Core Ops, SparseCore 0:
  11.4 538.1 all-reduce.1
where the time goes:
time: 635 us
  waiting for transfers between devices  534 us (84%)
  matrix products  40.1 us (6%)
  other arithmetic  24.9 us (4%)
  between operations  14.9 us (2%)
  starting transfers between devices  12.1 us (2%)
  local copies, waits for them, and re-layouts  8.4 us (1%)
    psum x1, waiting for transfers between devices, broadcast(): return lax.psum(kept, axis)  526 us
    dot_general x8, matrix products, partial_softmax(): jnp.dot(weights, value_rows, preferred_element_type=jnp.float32)  20.2 us
    dot_general x8, matrix products, partial_softmax(): lax.dot_general(query_head, key_rows, (((1,), (1,)), ((), ())), preferred...  19.9 us
    reduce_sum x8, other arithmetic, partial_softmax(): totals = jnp.sum(expons, axis=1, keepdims=True)  18.4 us
  transfers between devices with their start and end apart: 4, of which 2 were waited for; matrix products, arithmetic and copies ran while one was open for 1% of the time, Pallas kernels for 0%

commit v1 on v0

v1 whole, which is shorter than its diff:
```python
import functools
import math

import jax
import jax.numpy as jnp
from jax import lax
from jax.experimental import pallas as pl
from jax.experimental.pallas import tpu as pltpu
from jax.sharding import PartitionSpec as P

HD = 128
NEG = -1e30
LOG2E = 1.4426950408889634
MESH = pl.DeviceIdType.MESH
QT = 256


def ring_offset(j, n):
    odd = j % 2
    return odd * ((j + 1) // 2) + (1 - odd) * (n - j // 2)


def kernel(
    dims,
    owner_ref, clen_ref, q_ref, ckv_ref, skv_ref, slen_ref, pool_ref,
    out_ref,
    r1, x2, r2, x3, instr, prev, plen, m_ref, l_ref, acc_ref,
    s1, v1, s2, v2, s3, v3, sy, vy, sk, vk, sp, vp,
):
    nz, ns, nt = dims
    c = lax.axis_index("call")
    t = lax.axis_index("tensor")
    z = c // ns
    s = c % ns
    ncall = nz * ns
    plane = ns * nt
    me = s * nt + t
    heads = q_ref.shape[1] // HD
    rows = q_ref.shape[0]
    nq = rows // QT
    scale2 = LOG2E / math.sqrt(HD)

    def plane_dev(p):
        return (z * ns + p // nt, p % nt)

    def rcopy(src, dst, ssem, rsem, dev):
        return pltpu.make_async_remote_copy(
            src_ref=src, dst_ref=dst, send_sem=ssem, recv_sem=rsem,
            device_id=dev, device_id_type=MESH,
        )

    barrier = pltpu.get_barrier_semaphore()

    @pl.loop(1, plane)
    def _(j):
        pl.semaphore_signal(barrier, inc=1, device_id=plane_dev((me + j) % plane), device_id_type=MESH)

    @pl.loop(1, nz)
    def _(j):
        pl.semaphore_signal(
            barrier, inc=1, device_id=(((z + j) % nz) * ns + s, t), device_id_type=MESH
        )

    nxt = ((c + 1) % ncall, t)
    prv = ((c + ncall - 1) % ncall, t)
    pl.semaphore_signal(barrier, inc=1, device_id=nxt, device_id_type=MESH)
    pl.semaphore_signal(barrier, inc=1, device_id=prv, device_id_type=MESH)

    def own_part(h):
        col = pl.multiple_of(h * HD, HD)
        for i in range(nq):
            n = (i + 1) * QT
            rs = slice(i * QT, (i + 1) * QT)
            q = q_ref[rs, pl.ds(col, HD)]
            k = ckv_ref[0, 0:n, :]
            v = ckv_ref[1, 0:n, :]
            sc = lax.dot_general(q, k, (((1,), (1,)), ((), ())), preferred_element_type=jnp.float32)
            r = lax.broadcasted_iota(jnp.int32, (QT, QT), 0)
            cc = lax.broadcasted_iota(jnp.int32, (QT, QT), 1)
            diag = jnp.where(cc <= r, sc[:, n - QT : n], NEG)
            if i > 0:
                sc = jnp.concatenate([sc[:, 0 : n - QT], diag], axis=1)
            else:
                sc = diag
            m = jnp.max(sc, axis=1, keepdims=True)
            p = jnp.exp2((sc - m) * scale2)
            l = jnp.sum(p, axis=1, keepdims=True)
            acc = jnp.dot(p.astype(jnp.bfloat16), v, preferred_element_type=jnp.float32)
            m_ref[h, rs, :] = jnp.broadcast_to(m, (QT, HD))
            l_ref[h, rs, :] = jnp.broadcast_to(l, (QT, HD))
            acc_ref[h, rs, :] = acc

    def merge(h, i, sc, v):
        rs = slice(i * QT, (i + 1) * QT)
        m0 = m_ref[h, rs, :][:, 0:1]
        m = jnp.maximum(m0, jnp.max(sc, axis=1, keepdims=True))
        p = jnp.exp2((sc - m) * scale2)
        a = jnp.exp2((m0 - m) * scale2)
        l = l_ref[h, rs, :][:, 0:1] * a + jnp.sum(p, axis=1, keepdims=True)
        acc = acc_ref[h, rs, :] * a + jnp.dot(
            p.astype(jnp.bfloat16), v, preferred_element_type=jnp.float32
        )
        return m, l, acc

    def prev_part(h):
        col = pl.multiple_of(h * HD, HD)
        ns_ = prev.shape[1]
        ln = jnp.where(c > 0, plen[0:1, 0:1], 0)
        bias = jnp.where(lax.broadcasted_iota(jnp.int32, (1, ns_), 1) < ln, 0.0, NEG)
        for i in range(nq):
            rs = slice(i * QT, (i + 1) * QT)
            q = q_ref[rs, pl.ds(col, HD)]
            sc = lax.dot_general(
                q, prev[0], (((1,), (1,)), ((), ())), preferred_element_type=jnp.float32
            )
            m, l, acc = merge(h, i, jnp.where(bias < -1.0, NEG, sc), prev[1])
            m_ref[h, rs, :] = jnp.broadcast_to(m, (QT, HD))
            l_ref[h, rs, :] = jnp.broadcast_to(l, (QT, HD))
            acc_ref[h, rs, :] = acc

    def instr_part(h):
        col = pl.multiple_of(h * HD, HD)
        count = ns * nz * instr.shape[3]
        k = instr[:, :, 0].reshape(count, HD)
        v = instr[:, :, 1].reshape(count, HD)
        for i in range(nq):
            rs = slice(i * QT, (i + 1) * QT)
            q = q_ref[rs, pl.ds(col, HD)]
            sc = lax.dot_general(q, k, (((1,), (1,)), ((), ())), preferred_element_type=jnp.float32)
            m, l, acc = merge(h, i, sc, v)
            pos = lax.broadcasted_iota(jnp.int32, (QT, HD), 0) + i * QT
            res = jnp.where(pos < clen_ref[0], acc / l, 0.0)
            out_ref[rs, pl.ds(col, HD)] = res.astype(jnp.bfloat16)

    pl.semaphore_wait(barrier, plane - 1 + nz - 1 + 2)

    def p1(j):
        dst = (me + j) % plane
        return rcopy(
            pool_ref.at[dst % nt, dst // nt], r1.at[s, t], s1.at[j], v1.at[j], plane_dev(dst)
        )

    def p1_in(j):
        src = (me + plane - j) % plane
        return rcopy(
            pool_ref.at[0, 0], r1.at[src // nt, src % nt], s1.at[j], v1.at[j], plane_dev(src)
        )

    @pl.loop(1, plane)
    def _(j):
        p1(j).start()

    pk = rcopy(skv_ref, prev, sp.at[0], vp.at[0], nxt)
    pn = rcopy(slen_ref, plen, sp.at[1], vp.at[1], nxt)
    pk.start()
    pn.start()
    r1[s, t] = pool_ref[t, s]

    @pl.loop(0, heads)
    def _(h):
        own_part(h)

    @pl.loop(1, plane)
    def _(j):
        p1_in(j).wait_recv()

    owner = owner_ref[0]
    owner_s = owner % ns
    owner_z = owner // ns
    for b in range(nt):
        for f in range(nz // nt):
            per = x2.shape[2]
            x2[b * (nz // nt) + f] = r1[owner_s, b, :, f * per : (f + 1) * per, :]

    def p2(j):
        o = (z + ring_offset(j, nz)) % nz
        return rcopy(x2.at[o], r2.at[z], s2.at[j], v2.at[j], (o * ns + s, t))

    def p2_in(j):
        o = (z + nz - ring_offset(j, nz)) % nz
        return rcopy(x2.at[0], r2.at[o], s2.at[j], v2.at[j], (o * ns + s, t))

    @pl.loop(1, nz)
    def _(j):
        p2(j).start()

    r2[z] = x2[z]
    pk.wait_recv()
    pn.wait_recv()

    @pl.loop(0, heads)
    def _(h):
        prev_part(h)

    @pl.loop(1, nz)
    def _(j):
        p2_in(j).wait_recv()

    share = r2[owner_z]
    x3[...] = share
    instr[s, z] = share

    def p3(j):
        o = (z + ring_offset(j, nz)) % nz
        return rcopy(x3, instr.at[s, z], s3.at[j], v3.at[j], (o * ns + s, t))

    def p3_in(j):
        o = (z + nz - ring_offset(j, nz)) % nz
        return rcopy(x3, instr.at[s, o], s3.at[j], v3.at[j], (o * ns + s, t))

    @pl.loop(1, nz)
    def _(j):
        p3(j).start()

    sh = ns // 2
    mate_k = (z * ns + (s // 2) * 2 + 1 - s % 2, t)
    mate_y = (z * ns + (s + sh) % ns, t)
    s_k = (s // 2) * 2 + 1 - s % 2
    s_y = (s + sh) % ns
    s_d = (s_k + sh) % ns

    def slot(j):
        return (z + nz - ring_offset(j, nz)) % nz

    def to_y(j):
        return rcopy(instr.at[s, slot(j)], instr.at[s, slot(j)], sy.at[j], vy.at[j], mate_y)

    def from_y(j):
        return rcopy(instr.at[s_y, slot(j)], instr.at[s_y, slot(j)], sy.at[j], vy.at[j], mate_y)

    def to_k(a, w, j):
        return rcopy(instr.at[a, slot(j)], instr.at[a, slot(j)], sk.at[w, j], vk.at[w, j], mate_k)

    to_y(0).start()
    to_k(s, 0, 0).start()

    @pl.loop(1, nz)
    def _(j):
        p3_in(j).wait_recv()
        to_y(j).start()
        to_k(s, 0, j).start()

    @pl.loop(0, nz)
    def _(j):
        from_y(j).wait_recv()
        to_k(s_y, 1, j).start()

    @pl.loop(0, nz)
    def _(j):
        to_k(s_k, 0, j).wait_recv()
        to_k(s_d, 1, j).wait_recv()

    @pl.loop(0, heads)
    def _(h):
        instr_part(h)

    @pl.loop(1, plane)
    def _(j):
        p1(j).wait_send()

    pk.wait_send()
    pn.wait_send()

    @pl.loop(1, nz)
    def _(j):
        p2(j).wait_send()
        p3(j).wait_send()

    @pl.loop(0, nz)
    def _(j):
        to_y(j).wait_send()
        to_k(s, 0, j).wait_send()
        to_k(s_y, 1, j).wait_send()


def shards(dims, queries, child_kv, summ_kv, instr_pool, child_len, summ_len, owner_group):
    nz, ns, nt = dims
    rows, width = queries.shape[1], queries.shape[2]
    heads = width // HD
    block = instr_pool.shape[1]
    summ = summ_kv.shape[2]
    quarter = block // ns
    pool = instr_pool[0].reshape(ns, quarter, 2, nt, HD).transpose(3, 0, 2, 1, 4)
    slen = jnp.broadcast_to(summ_len[0], (8, 128)).astype(jnp.int32)
    piece = quarter * nt // nz
    vm = pl.BlockSpec(memory_space=pltpu.VMEM)
    sm = pl.BlockSpec(memory_space=pltpu.SMEM)
    bf = jnp.bfloat16
    dma = pltpu.SemaphoreType.DMA
    out = pl.pallas_call(
        functools.partial(kernel, dims),
        name="merge_attention",
        out_shape=jax.ShapeDtypeStruct((rows, width), bf),
        in_specs=[sm, sm, vm, vm, vm, vm, vm],
        out_specs=vm,
        scratch_shapes=[
            pltpu.VMEM((ns, nt, 2, quarter, HD), bf),
            pltpu.VMEM((nz, 2, piece, HD), bf),
            pltpu.VMEM((nz, 2, piece, HD), bf),
            pltpu.VMEM((2, piece, HD), bf),
            pltpu.VMEM((ns, nz, 2, piece, HD), bf),
            pltpu.VMEM((2, summ, HD), bf),
            pltpu.VMEM((8, 128), jnp.int32),
            pltpu.VMEM((heads, rows, HD), jnp.float32),
            pltpu.VMEM((heads, rows, HD), jnp.float32),
            pltpu.VMEM((heads, rows, HD), jnp.float32),
            dma((ns * nt,)), dma((ns * nt,)),
            dma((nz,)), dma((nz,)),
            dma((nz,)), dma((nz,)),
            dma((nz,)), dma((nz,)),
            dma((2, nz)), dma((2, nz)),
            dma((2,)), dma((2,)),
        ],
        compiler_params=pltpu.CompilerParams(
            collective_id=0, has_side_effects=True, vmem_limit_bytes=56 * 1024 * 1024
        ),
    )(owner_group, child_len, queries[0], child_kv[0], summ_kv[0], slen, pool)
    return out[None]


def solution(mesh):
    sizes = dict(mesh.shape)
    ns = 4
    dims = (sizes["call"] // ns, ns, sizes["tensor"])
    in_specs = (
        P("call", None, "tensor"),
        P("call", None, None, "tensor"),
        P("call", None, None, "tensor"),
        P("call", "tensor", None, None),
        P("call"),
        P("call"),
        P(),
    )
    out_specs = P("call", None, "tensor")
    return jax.shard_map(
        functools.partial(shards, dims), mesh=mesh, in_specs=in_specs, out_specs=out_specs, check_vma=False
    )
```

time: 635 us -> 87.2 us (0.14)
  waiting for transfers between devices: 534 us -> 0 us
  Pallas kernels: 0 us -> 79.4 us
  matrix products: 40.1 us -> 0 us
  other arithmetic: 24.9 us -> 0 us
  between operations: 14.9 us -> 1.95 us
  starting transfers between devices: 12.1 us -> 0 us
    psum x1 -> x0, waiting for transfers between devices: 526 us -> none  [broadcast(): return lax.psum(kept, axis)]
    pallas_call x0 -> x1, Pallas kernels: none -> 79.4 us  [shards(): pl.pallas_call(functools.partial(kernel, dims), name='merge_attention', o...]
    dot_general x16 -> x0, matrix products: 40.1 us -> none  [the longest x8 20.2 us: partial_softmax(): jnp.dot(weights, value_rows, preferred_element_type=jnp.float32)]
    reduce_sum x8 -> x0, other arithmetic: 18.4 us -> none  [partial_softmax(): totals = jnp.sum(expons, axis=1, keepdims=True)]
    ppermute x2 -> x0, starting transfers between devices: 8.13 us -> none  [passed_along(): return lax.ppermute(block, axis, route)]
    all_to_all x1 -> x0, waiting for transfers between devices: 8.02 us -> none  [shards(): lax.all_to_all(fetched, 'tensor', split_axis=3, concat_axis=1, tiled=True)]
  transfers between devices with their start and end apart: 4 -> 0, of which waited for: 2 -> 0; matrix products, arithmetic and copies ran while one was open for 1% -> 0% of each run, Pallas kernels for 0% -> 0%
where the time goes in v1:
time: 87.2 us; the launch traced here: 86.9 us
  Pallas kernels  79.4 us (91%)
  local copies, waits for them, and re-layouts  5.57 us (6%)
  between operations  1.95 us (2%)
    pallas_call x1, Pallas kernels, shards(): pl.pallas_call(functools.partial(kernel, dims), name='merge_attention', o...  79.4 us
    unnamed x1, local copies, waits for them, and re-layouts  2.67 us
    another operation x2, local copies, waits for them, and re-layouts, shards(): instr_pool[0].reshape(ns, quarter, 2, nt, HD).transpose(3, 0, 2, 1, 4)  2.31 us

profile of v1, /device:TPU:1, one launch (start us, length us, event | category | flops | bytes accessed | tf_op | source)
XLA Modules:
  0.0 86.9 jit_solution(4753837279774574961)
XLA Ops:
  1.9 0.6 broadcast_in_dim.6.slen_ref
  2.5 1.4 %reshape = bf16[4,32,2,8,128]{4,3,2,1,0:T(8,128)(2,1)S(1)} reshape(bf16[1,128,2,1024]{3,2,1,0:T(2,128)(2,1)} %param.10) | data formatting | bytes 1048576 | tf_op jit(solution)/shard_map/reshape;squeeze | solution.py:283
  3.9 0.9 %copy.13 = bf16[4,32,2,8,128]{4,1,2,0,3:T(8,128)(2,1)} copy(bf16[4,32,2,8,128]{4,3,2,1,0:T(8,128)(2,1)S(1)} %reshape) | data formatting | bytes 1048576 | tf_op jit(solution)/shard_map/reshape;squeeze | solution.py:283
  4.8 79.4 %merge_attention.1 = bf16[768,1024]{1,0:T(8,128)(2,1)} custom-call(s32[1]{0:T(128)S(6)} %copy.17.owner_ref, s32[1]{0:T(128)S(6)} %copy.15.clen_ref, bf16[768,1024]{1,0:T(8,128)(2,1)} %bitcast.11, bf16[2,768,128]{2,1,0:T(8,128)(2,1)} %bitcast.12, bf16[2,256,128]{2,1,0:T(8,128)(2,1)} %bitcast.13, s32[8,128]{1,0:T(8,128)} %broadcast_in_dim.6.slen_ref, ...), custom_call_target="tpu_custom_call" | custom-call | tf_op jit(solution)/shard_map/merge_attention/pallas_call | solution.py:290
  84.2 2.7 %copy.18 = bf16[1,768,1024]{2,1,0:T(8,128)(2,1)} copy(bf16[1,768,1024]{2,1,0:T(8,128)(2,1)} %bitcast.9) | data formatting | bytes 3145728

commit v2 on v1

--- a/solution.py
+++ b/solution.py
@@ -24,7 +24,7 @@
     dims,
     owner_ref, clen_ref, q_ref, ckv_ref, skv_ref, slen_ref, pool_ref,
     out_ref,
-    r1, x2, r2, x3, instr, prev, plen, m_ref, l_ref, acc_ref,
+    r1, x2, r2, x3, instr, prev, plen, mlen, m_ref, acc_ref,
     s1, v1, s2, v2, s3, v3, sy, vy, sk, vk, sp, vp,
 ):
     nz, ns, nt = dims
@@ -66,84 +66,105 @@
     pl.semaphore_signal(barrier, inc=1, device_id=nxt, device_id_type=MESH)
     pl.semaphore_signal(barrier, inc=1, device_id=prv, device_id_type=MESH)
 
+    def dot_t(a, b):
+        return lax.dot_general(a, b, (((1,), (1,)), ((), ())), preferred_element_type=jnp.float32)
+
+    def with_ones(v):
+        return jnp.concatenate([v, jnp.ones_like(v)], axis=1)
+
+    def wide(m, n):
+        return jnp.concatenate([m] * (n // HD), axis=1)
+
+    def row_max(sc):
+        return jnp.broadcast_to(jnp.max(sc, axis=1, keepdims=True), (QT, HD))
+
+    def weights(sc, m):
+        return jnp.exp2((sc - wide(m, sc.shape[1])) * scale2).astype(jnp.bfloat16)
+
+    def rows_of(i):
+        return slice(i * QT, (i + 1) * QT)
+
+    def q_tile(h, i):
+        return q_ref[rows_of(i), pl.ds(pl.multiple_of(h * HD, HD), HD)]
+
     def own_part(h):
-        col = pl.multiple_of(h * HD, HD)
+        r = lax.broadcasted_iota(jnp.int32, (QT, QT), 0)
+        cc = lax.broadcasted_iota(jnp.int32, (QT, QT), 1)
         for i in range(nq):
             n = (i + 1) * QT
-            rs = slice(i * QT, (i + 1) * QT)
-            q = q_ref[rs, pl.ds(col, HD)]
-            k = ckv_ref[0, 0:n, :]
-            v = ckv_ref[1, 0:n, :]
-            sc = lax.dot_general(q, k, (((1,), (1,)), ((), ())), preferred_element_type=jnp.float32)
-            r = lax.broadcasted_iota(jnp.int32, (QT, QT), 0)
-            cc = lax.broadcasted_iota(jnp.int32, (QT, QT), 1)
+            sc = dot_t(q_tile(h, i), ckv_ref[0, 0:n, :])
             diag = jnp.where(cc <= r, sc[:, n - QT : n], NEG)
             if i > 0:
                 sc = jnp.concatenate([sc[:, 0 : n - QT], diag], axis=1)
             else:
                 sc = diag
-            m = jnp.max(sc, axis=1, keepdims=True)
-            p = jnp.exp2((sc - m) * scale2)
-            l = jnp.sum(p, axis=1, keepdims=True)
-            acc = jnp.dot(p.astype(jnp.bfloat16), v, preferred_element_type=jnp.float32)
-            m_ref[h, rs, :] = jnp.broadcast_to(m, (QT, HD))
-            l_ref[h, rs, :] = jnp.broadcast_to(l, (QT, HD))
-            acc_ref[h, rs, :] = acc
-
-    def merge(h, i, sc, v):
-        rs = slice(i * QT, (i + 1) * QT)
-        m0 = m_ref[h, rs, :][:, 0:1]
-        m = jnp.maximum(m0, jnp.max(sc, axis=1, keepdims=True))
-        p = jnp.exp2((sc - m) * scale2)
+            m = row_max(sc)
+            m_ref[h, rows_of(i), :] = m
+            acc_ref[h, rows_of(i), :] = jnp.dot(
+                weights(sc, m), with_ones(ckv_ref[1, 0:n, :]), preferred_element_type=jnp.float32
+            )
+
+    def merge(h, i, sc, v2):
+        m0 = m_ref[h, rows_of(i), :]
+        m = jnp.maximum(m0, row_max(sc))
         a = jnp.exp2((m0 - m) * scale2)
-        l = l_ref[h, rs, :][:, 0:1] * a + jnp.sum(p, axis=1, keepdims=True)
-        acc = acc_ref[h, rs, :] * a + jnp.dot(
-            p.astype(jnp.bfloat16), v, preferred_element_type=jnp.float32
-        )
-        return m, l, acc
+        acc = acc_ref[h, rows_of(i), :] * wide(a, 2 * HD) + jnp.dot(
+            weights(sc, m), v2, preferred_element_type=jnp.float32
+        )
+        return m, acc
 
     def prev_part(h):
-        col = pl.multiple_of(h * HD, HD)
-        ns_ = prev.shape[1]
+        count = prev.shape[1]
         ln = jnp.where(c > 0, plen[0:1, 0:1], 0)
-        bias = jnp.where(lax.broadcasted_iota(jnp.int32, (1, ns_), 1) < ln, 0.0, NEG)
+        ok = jnp.broadcast_to(
+            lax.broadcasted_iota(jnp.int32, (1, count), 1) < ln, (QT, count)
+        )
+        v2 = with_ones(prev[1])
         for i in range(nq):
-            rs = slice(i * QT, (i + 1) * QT)
-            q = q_ref[rs, pl.ds(col, HD)]
-            sc = lax.dot_general(
-                q, prev[0], (((1,), (1,)), ((), ())), preferred_element_type=jnp.float32
-            )
-            m, l, acc = merge(h, i, jnp.where(bias < -1.0, NEG, sc), prev[1])
-            m_ref[h, rs, :] = jnp.broadcast_to(m, (QT, HD))
-            l_ref[h, rs, :] = jnp.broadcast_to(l, (QT, HD))
-            acc_ref[h, rs, :] = acc
-
-    def instr_part(h):
-        col = pl.multiple_of(h * HD, HD)
-        count = ns * nz * instr.shape[3]
-        k = instr[:, :, 0].reshape(count, HD)
-        v = instr[:, :, 1].reshape(count, HD)
+            sc = jnp.where(ok, dot_t(q_tile(h, i), prev[0]), NEG)
+            m, acc = merge(h, i, sc, v2)
+            m_ref[h, rows_of(i), :] = m
+            acc_ref[h, rows_of(i), :] = acc
+
+    def instr_part(h, qa, qb, last):
+        count = nz * instr.shape[3]
+        k = jnp.concatenate([instr[x, :, 0].reshape(count, HD) for x in (qa, qb)], axis=0)
+        v2 = with_ones(
+            jnp.concatenate([instr[x, :, 1].reshape(count, HD) for x in (qa, qb)], axis=0)
+        )
         for i in range(nq):
-            rs = slice(i * QT, (i + 1) * QT)
-            q = q_ref[rs, pl.ds(col, HD)]
-            sc = lax.dot_general(q, k, (((1,), (1,)), ((), ())), preferred_element_type=jnp.float32)
-            m, l, acc = merge(h, i, sc, v)
-            pos = lax.broadcasted_iota(jnp.int32, (QT, HD), 0) + i * QT
-            res = jnp.where(pos < clen_ref[0], acc / l, 0.0)
-            out_ref[rs, pl.ds(col, HD)] = res.astype(jnp.bfloat16)
-
+            m, acc = merge(h, i, dot_t(q_tile(h, i), k), v2)
+            if last:
+                pos = lax.broadcasted_iota(jnp.int32, (QT, HD), 0) + i * QT
+                res = jnp.where(pos < clen_ref[0], acc[:, :HD] / acc[:, HD:], 0.0)
+                out_ref[rows_of(i), pl.ds(pl.multiple_of(h * HD, HD), HD)] = res.astype(
+                    jnp.bfloat16
+                )
+            else:
+                m_ref[h, rows_of(i), :] = m
+                acc_ref[h, rows_of(i), :] = acc
+
+    mlen[...] = jnp.full((8, 128), slen_ref[0], jnp.int32)
     pl.semaphore_wait(barrier, plane - 1 + nz - 1 + 2)
+
+    def pool_piece(h, part):
+        quarter = r1.shape[3]
+        return pool_ref.at[
+            :,
+            pl.ds(pl.multiple_of(part * quarter, quarter), quarter),
+            pl.ds(pl.multiple_of(h * HD, HD), HD),
+        ]
 
     def p1(j):
         dst = (me + j) % plane
         return rcopy(
-            pool_ref.at[dst % nt, dst // nt], r1.at[s, t], s1.at[j], v1.at[j], plane_dev(dst)
+            pool_piece(dst % nt, dst // nt), r1.at[s, t], s1.at[j], v1.at[j], plane_dev(dst)
         )
 
     def p1_in(j):
         src = (me + plane - j) % plane
         return rcopy(
-            pool_ref.at[0, 0], r1.at[src // nt, src % nt], s1.at[j], v1.at[j], plane_dev(src)
+            r1.at[0, 0], r1.at[src // nt, src % nt], s1.at[j], v1.at[j], plane_dev(src)
         )
 
     @pl.loop(1, plane)
@@ -151,12 +172,12 @@
         p1(j).start()
 
     pk = rcopy(skv_ref, prev, sp.at[0], vp.at[0], nxt)
-    pn = rcopy(slen_ref, plen, sp.at[1], vp.at[1], nxt)
+    pn = rcopy(mlen, plen, sp.at[1], vp.at[1], nxt)
     pk.start()
     pn.start()
-    r1[s, t] = pool_ref[t, s]
-
-    @pl.loop(0, heads)
+    r1[s, t] = pool_piece(t, s)[...]
+
+    @pl.loop(0, heads // 2)
     def _(h):
         own_part(h)
 
@@ -182,15 +203,12 @@
 
     @pl.loop(1, nz)
     def _(j):
-        p2(j).start()
+        p2(nz - j).start()
 
     r2[z] = x2[z]
-    pk.wait_recv()
-    pn.wait_recv()
-
-    @pl.loop(0, heads)
-    def _(h):
-        prev_part(h)
+    @pl.loop(heads // 2, heads)
+    def _(h):
+        own_part(h)
 
     @pl.loop(1, nz)
     def _(j):
@@ -210,7 +228,14 @@
 
     @pl.loop(1, nz)
     def _(j):
-        p3(j).start()
+        p3(nz - j).start()
+
+    pk.wait_recv()
+    pn.wait_recv()
+
+    @pl.loop(0, heads)
+    def _(h):
+        prev_part(h)
 
     sh = ns // 2
     mate_k = (z * ns + (s // 2) * 2 + 1 - s % 2, t)
@@ -242,17 +267,28 @@
 
     @pl.loop(0, nz)
     def _(j):
+        to_k(s_k, 0, j).wait_recv()
+
+    @pl.loop(0, heads // 2)
+    def _(h):
+        instr_part(h, s, s_k, False)
+
+    @pl.loop(0, nz)
+    def _(j):
         from_y(j).wait_recv()
         to_k(s_y, 1, j).start()
 
+    @pl.loop(heads // 2, heads)
+    def _(h):
+        instr_part(h, s, s_k, False)
+
     @pl.loop(0, nz)
     def _(j):
-        to_k(s_k, 0, j).wait_recv()
         to_k(s_d, 1, j).wait_recv()
 
     @pl.loop(0, heads)
     def _(h):
-        instr_part(h)
+        instr_part(h, s_y, s_d, True)
 
     @pl.loop(1, plane)
     def _(j):
@@ -280,8 +316,7 @@
     block = instr_pool.shape[1]
     summ = summ_kv.shape[2]
     quarter = block // ns
-    pool = instr_pool[0].reshape(ns, quarter, 2, nt, HD).transpose(3, 0, 2, 1, 4)
-    slen = jnp.broadcast_to(summ_len[0], (8, 128)).astype(jnp.int32)
+    pool = instr_pool[0].transpose(1, 0, 2)
     piece = quarter * nt // nz
     vm = pl.BlockSpec(memory_space=pltpu.VMEM)
     sm = pl.BlockSpec(memory_space=pltpu.SMEM)
@@ -291,7 +326,7 @@
         functools.partial(kernel, dims),
         name="merge_attention",
         out_shape=jax.ShapeDtypeStruct((rows, width), bf),
-        in_specs=[sm, sm, vm, vm, vm, vm, vm],
+        in_specs=[sm, sm, vm, vm, vm, sm, vm],
         out_specs=vm,
         scratch_shapes=[
             pltpu.VMEM((ns, nt, 2, quarter, HD), bf),
@@ -301,9 +336,9 @@
             pltpu.VMEM((ns, nz, 2, piece, HD), bf),
             pltpu.VMEM((2, summ, HD), bf),
             pltpu.VMEM((8, 128), jnp.int32),
+            pltpu.VMEM((8, 128), jnp.int32),
             pltpu.VMEM((heads, rows, HD), jnp.float32),
-            pltpu.VMEM((heads, rows, HD), jnp.float32),
-            pltpu.VMEM((heads, rows, HD), jnp.float32),
+            pltpu.VMEM((heads, rows, 2 * HD), jnp.float32),
             dma((ns * nt,)), dma((ns * nt,)),
             dma((nz,)), dma((nz,)),
             dma((nz,)), dma((nz,)),
@@ -314,7 +349,7 @@
         compiler_params=pltpu.CompilerParams(
             collective_id=0, has_side_effects=True, vmem_limit_bytes=56 * 1024 * 1024
         ),
-    )(owner_group, child_len, queries[0], child_kv[0], summ_kv[0], slen, pool)
+    )(owner_group, child_len, queries[0], child_kv[0], summ_kv[0], summ_len, pool)
     return out[None]
 
 

time: 87.2 us -> 71.8 us (0.82)
  Pallas kernels: 79.4 us -> 64.9 us
  local copies, waits for them, and re-layouts: 5.57 us -> 4.62 us
    pallas_call x1, Pallas kernels: 79.4 us -> 64.9 us  [shards(): pl.pallas_call(functools.partial(kernel, dims), name='merge_attention', o...]
    another operation x2 -> x0, local copies, waits for them, and re-layouts: 2.31 us -> none  [shards(): instr_pool[0].reshape(ns, quarter, 2, nt, HD).transpose(3, 0, 2, 1, 4)]
    unnamed x1 -> x2, local copies, waits for them, and re-layouts: 2.67 us -> 4.62 us
where the time goes in v2:
time: 71.8 us; the launch traced here: 71.5 us
  Pallas kernels  64.9 us (90%)
  local copies, waits for them, and re-layouts  4.62 us (6%)
  between operations  1.95 us (3%)
    pallas_call x1, Pallas kernels, shards(): pl.pallas_call(functools.partial(kernel, dims), name='merge_attention', o...  64.9 us
    unnamed x2, local copies, waits for them, and re-layouts  4.62 us

profile of v2, /device:TPU:1, one launch (start us, length us, event | category | flops | bytes accessed | tf_op | source)
XLA Modules:
  0.0 71.5 jit_solution(4804337660371809871)
XLA Ops:
  1.9 2.0 %copy.10 = bf16[1,128,2,1024]{3,1,2,0:T(8,128)(2,1)} copy(bf16[1,128,2,1024]{3,2,1,0:T(2,128)(2,1)} %param.10) | data formatting | bytes 1048576 | tf_op args[3]
  3.9 64.9 %merge_attention.1 = bf16[768,1024]{1,0:T(8,128)(2,1)} custom-call(s32[1]{0:T(128)S(6)} %copy.14.owner_ref, s32[1]{0:T(128)S(6)} %copy.12.clen_ref, bf16[768,1024]{1,0:T(8,128)(2,1)} %bitcast.11, bf16[2,768,128]{2,1,0:T(8,128)(2,1)} %bitcast.12, bf16[2,256,128]{2,1,0:T(8,128)(2,1)} %bitcast.13, s32[1]{0:T(128)S(6)} %copy.13.slen_ref, ...), custom_call_target="tpu_custom_call" | custom-call | tf_op jit(solution)/shard_map/merge_attention/pallas_call | solution.py:325
  68.8 2.7 %copy.15 = bf16[1,768,1024]{2,1,0:T(8,128)(2,1)} copy(bf16[1,768,1024]{2,1,0:T(8,128)(2,1)} %bitcast.9) | data formatting | bytes 3145728

commit v3 on v2

--- a/solution.py
+++ b/solution.py
@@ -22,10 +22,10 @@
 
 def kernel(
     dims,
-    owner_ref, clen_ref, q_ref, ckv_ref, skv_ref, slen_ref, pool_ref,
+    owner_ref, clen_ref, q_hbm, ckv_hbm, skv_ref, slen_ref, pool_ref,
     out_ref,
-    r1, x2, r2, x3, instr, prev, plen, mlen, m_ref, acc_ref,
-    s1, v1, s2, v2, s3, v3, sy, vy, sk, vk, sp, vp,
+    r1, x2, r2, x3, instr, prev, plen, mlen, m_ref, acc_ref, q_ref, ckv_ref,
+    s1, v1, s2, v2, s3, v3, sy, vy, sk, vk, sp, vp, ld,
 ):
     nz, ns, nt = dims
     c = lax.axis_index("call")
@@ -90,9 +90,10 @@
     def own_part(h):
         r = lax.broadcasted_iota(jnp.int32, (QT, QT), 0)
         cc = lax.broadcasted_iota(jnp.int32, (QT, QT), 1)
+        scores = [dot_t(q_tile(h, i), ckv_ref[0, 0 : (i + 1) * QT, :]) for i in range(nq)]
         for i in range(nq):
             n = (i + 1) * QT
-            sc = dot_t(q_tile(h, i), ckv_ref[0, 0:n, :])
+            sc = scores[i]
             diag = jnp.where(cc <= r, sc[:, n - QT : n], NEG)
             if i > 0:
                 sc = jnp.concatenate([sc[:, 0 : n - QT], diag], axis=1)
@@ -120,8 +121,9 @@
             lax.broadcasted_iota(jnp.int32, (1, count), 1) < ln, (QT, count)
         )
         v2 = with_ones(prev[1])
+        scores = [dot_t(q_tile(h, i), prev[0]) for i in range(nq)]
         for i in range(nq):
-            sc = jnp.where(ok, dot_t(q_tile(h, i), prev[0]), NEG)
+            sc = jnp.where(ok, scores[i], NEG)
             m, acc = merge(h, i, sc, v2)
             m_ref[h, rows_of(i), :] = m
             acc_ref[h, rows_of(i), :] = acc
@@ -132,8 +134,9 @@
         v2 = with_ones(
             jnp.concatenate([instr[x, :, 1].reshape(count, HD) for x in (qa, qb)], axis=0)
         )
+        scores = [dot_t(q_tile(h, i), k) for i in range(nq)]
         for i in range(nq):
-            m, acc = merge(h, i, dot_t(q_tile(h, i), k), v2)
+            m, acc = merge(h, i, scores[i], v2)
             if last:
                 pos = lax.broadcasted_iota(jnp.int32, (QT, HD), 0) + i * QT
                 res = jnp.where(pos < clen_ref[0], acc[:, :HD] / acc[:, HD:], 0.0)
@@ -144,6 +147,10 @@
                 m_ref[h, rows_of(i), :] = m
                 acc_ref[h, rows_of(i), :] = acc
 
+    load_q = pltpu.make_async_copy(q_hbm, q_ref, ld.at[0])
+    load_kv = pltpu.make_async_copy(ckv_hbm, ckv_ref, ld.at[1])
+    load_q.start()
+    load_kv.start()
     mlen[...] = jnp.full((8, 128), slen_ref[0], jnp.int32)
     pl.semaphore_wait(barrier, plane - 1 + nz - 1 + 2)
 
@@ -175,7 +182,10 @@
     pn = rcopy(mlen, plen, sp.at[1], vp.at[1], nxt)
     pk.start()
     pn.start()
-    r1[s, t] = pool_piece(t, s)[...]
+    keep = pltpu.make_async_copy(pool_piece(t, s), r1.at[s, t], ld.at[2])
+    keep.start()
+    load_q.wait()
+    load_kv.wait()
 
     @pl.loop(0, heads // 2)
     def _(h):
@@ -185,6 +195,7 @@
     def _(j):
         p1_in(j).wait_recv()
 
+    keep.wait()
     owner = owner_ref[0]
     owner_s = owner % ns
     owner_z = owner // ns
@@ -320,13 +331,14 @@
     piece = quarter * nt // nz
     vm = pl.BlockSpec(memory_space=pltpu.VMEM)
     sm = pl.BlockSpec(memory_space=pltpu.SMEM)
+    hb = pl.BlockSpec(memory_space=pl.ANY)
     bf = jnp.bfloat16
     dma = pltpu.SemaphoreType.DMA
     out = pl.pallas_call(
         functools.partial(kernel, dims),
         name="merge_attention",
         out_shape=jax.ShapeDtypeStruct((rows, width), bf),
-        in_specs=[sm, sm, vm, vm, vm, sm, vm],
+        in_specs=[sm, sm, hb, hb, hb, sm, hb],
         out_specs=vm,
         scratch_shapes=[
             pltpu.VMEM((ns, nt, 2, quarter, HD), bf),
@@ -339,12 +351,15 @@
             pltpu.VMEM((8, 128), jnp.int32),
             pltpu.VMEM((heads, rows, HD), jnp.float32),
             pltpu.VMEM((heads, rows, 2 * HD), jnp.float32),
+            pltpu.VMEM((rows, width), bf),
+            pltpu.VMEM((2, rows, HD), bf),
             dma((ns * nt,)), dma((ns * nt,)),
             dma((nz,)), dma((nz,)),
             dma((nz,)), dma((nz,)),
             dma((nz,)), dma((nz,)),
             dma((2, nz)), dma((2, nz)),
             dma((2,)), dma((2,)),
+            dma((3,)),
         ],
         compiler_params=pltpu.CompilerParams(
             collective_id=0, has_side_effects=True, vmem_limit_bytes=56 * 1024 * 1024

time: 71.8 us -> 69.8 us (0.972)
  Pallas kernels: 64.9 us -> 63 us
    pallas_call x1, Pallas kernels: 64.9 us -> 63 us  [shards(): pl.pallas_call(functools.partial(kernel, dims), name='merge_attention', o...]
where the time goes in v3:
time: 69.8 us; the launch traced here: 69.6 us
  Pallas kernels  63 us (90%)
  local copies, waits for them, and re-layouts  4.62 us (7%)
  between operations  1.95 us (3%)
    pallas_call x1, Pallas kernels, shards(): pl.pallas_call(functools.partial(kernel, dims), name='merge_attention', o...  63 us
    unnamed x2, local copies, waits for them, and re-layouts  4.62 us

profile of v3, /device:TPU:1, one launch (start us, length us, event | category | flops | bytes accessed | tf_op | source)
XLA Modules:
  0.0 69.6 jit_solution(11145114528030052900)
XLA Ops:
  1.9 2.0 %copy.10 = bf16[1,128,2,1024]{3,1,2,0:T(8,128)(2,1)} copy(bf16[1,128,2,1024]{3,2,1,0:T(2,128)(2,1)} %param.10) | data formatting | bytes 1048576 | tf_op args[3]
  3.9 63.0 %merge_attention.1 = bf16[768,1024]{1,0:T(8,128)(2,1)} custom-call(s32[1]{0:T(128)S(6)} %copy.14.owner_ref, s32[1]{0:T(128)S(6)} %copy.12.clen_ref, bf16[768,1024]{1,0:T(8,128)(2,1)} %bitcast.11, bf16[2,768,128]{2,1,0:T(8,128)(2,1)} %bitcast.12, bf16[2,256,128]{2,1,0:T(8,128)(2,1)} %bitcast.13, s32[1]{0:T(128)S(6)} %copy.13.slen_ref, ...), custom_call_target="tpu_custom_call" | custom-call | tf_op jit(solution)/shard_map/merge_attention/pallas_call | solution.py:337
  66.9 2.7 %copy.15 = bf16[1,768,1024]{2,1,0:T(8,128)(2,1)} copy(bf16[1,768,1024]{2,1,0:T(8,128)(2,1)} %bitcast.9) | data formatting | bytes 3145728
